TPU v7x, 32 devices: a whole 2x2x4 slice. The times are simulated.
32 devices in a mesh: ctx: 2 (over x), tp: 4 (over y, core), pp: 4 (over z).
Axes of the slice: x: 2, y: 2, z: 4, core: 2. Of those that a mesh axis runs over, the one named last changes fastest.
Arguments:
- lin_query: bfloat16 [4, 512, 8192], P('pp', 'ctx', 'tp'), may hold values from -6 to 6
- lin_key: bfloat16 [4, 512, 8192], P('pp', 'ctx', 'tp'), may hold values from -6 to 6
- lin_value: bfloat16 [4, 512, 8192], P('pp', 'ctx', 'tp'), may hold values from -6 to 6
- log_decay: float32 [4, 512, 64], P('pp', 'ctx', 'tp'), may hold values from -1 to 0, as said below
- out_gate: bfloat16 [4, 512, 8192], P('pp', 'ctx', 'tp'), may hold values from -6 to 6
- norm_gain: float32 [4, 8192], P('pp', 'tp'), may hold values from 0.1 to 1.9
- soft_query: bfloat16 [4, 512, 8192], P('pp', 'ctx', 'tp'), may hold values from -5 to 5
- soft_key: bfloat16 [4, 512, 1024], P('pp', 'ctx', 'tp'), may hold values from -5 to 5
- soft_value: bfloat16 [4, 512, 1024], P('pp', 'ctx', 'tp'), may hold values from -6 to 6
Outputs:
- lin_handed: bfloat16 [4, 512, 8192], P('pp', 'ctx', 'tp')
- soft_handed: bfloat16 [4, 512, 8192], P('pp', 'ctx', 'tp')
Inputs may be any that keep to these rules, and one draw needn't show every extreme that they name: `log_decay`: negative everywhere.
All inputs are finite; a program needn't handle non-finite values.
Results may differ from a plain program's by a relative error of at most 0.0049.
Values may be sent and summed in bfloat16 or wider, within the bound.
No kernel may reach another device: no remote copies, remote signals or barrier semaphores. Data moves between devices by JAX's collectives and lax.ppermute only.
A program may use at most 128 MiB of HBM per device.

v0:
```python
import math
import jax
import jax.numpy as jnp
from jax import lax
from jax.sharding import PartitionSpec as P

HEADS = 64
KV_HEADS = 8
HD = 128
BLK = 256
epsilon = 1e-06
lowest = -1e30


def passed_along(block, axis, distance):
    devices = range(lax.axis_size(axis))
    route = [((i - distance) % len(devices), i) for i in devices]
    return lax.ppermute(block, axis, route)


def lightning_local(query_rows, key_rows, value_rows, decays):
    length, head_count = decays.shape
    blocks = length // BLK
    queries = query_rows.reshape(blocks, BLK, head_count, HD)
    keys_all = key_rows.reshape(blocks, BLK, head_count, HD)
    values_all = value_rows.reshape(blocks, BLK, head_count, HD)
    running_log = jnp.cumsum(decays.reshape(blocks, BLK, head_count), axis=1)
    closing_log = running_log[:, -1, :]
    scores = jnp.einsum("bthd,bshd->bhts", queries, keys_all, preferred_element_type=jnp.float32)
    log_turned = jnp.swapaxes(running_log, 1, 2)
    log_gap = log_turned[:, :, :, None] - log_turned[:, :, None, :]
    causal = lax.iota(jnp.int32, BLK)[:, None] >= lax.iota(jnp.int32, BLK)[None, :]
    decay_mask = jnp.where(causal, jnp.exp(jnp.where(causal, log_gap, 0.0)), 0.0)
    weights = (scores * decay_mask).astype(jnp.bfloat16)
    inside = jnp.einsum("bhts,bshd->bthd", weights, values_all, preferred_element_type=jnp.float32)
    pressed = (
        keys_all.astype(jnp.float32) * jnp.exp(closing_log[:, None, :] - running_log)[..., None]
    ).astype(jnp.bfloat16)
    updates = jnp.einsum("bshd,bshe->bhde", pressed, values_all, preferred_element_type=jnp.float32)

    def advance(state, inputs):
        factor_log, update = inputs
        return (jnp.exp(factor_log)[:, None, None] * state + update, state)

    closing, before = lax.scan(
        advance, jnp.zeros((head_count, HD, HD), jnp.float32), (closing_log, updates)
    )
    lifted = queries.astype(jnp.float32) * jnp.exp(running_log)[..., None]
    earlier_part = jnp.einsum("bthd,bhde->bthe", lifted, before, precision=lax.Precision.HIGHEST)
    offsets = jnp.cumsum(closing_log, axis=0) - closing_log
    carried = lifted * jnp.exp(offsets)[:, None, :, None]
    return (inside + earlier_part, carried, closing, jnp.sum(closing_log, axis=0))


def absorb(running, query_rows, row_pos, key_rows, value_rows, key_pos):
    row_peak, totals, weighted = running
    scores = jnp.einsum(
        "tkgd,skd->tkgs", query_rows, key_rows, preferred_element_type=jnp.float32
    ) * HD ** (-0.5)
    causal = (row_pos[:, None] >= key_pos[None, :])[:, None, None, :]
    block_peak = jnp.max(jnp.where(causal, scores, lowest), axis=-1)
    new_peak = jnp.maximum(row_peak, block_peak)
    unscaled = jnp.where(causal, jnp.exp(scores - new_peak[..., None]), 0.0)
    shrink = jnp.exp(row_peak - new_peak)
    totals = shrink * totals + jnp.sum(unscaled, axis=-1)
    weighted = shrink[..., None] * weighted + jnp.einsum(
        "tkgs,skd->tkgd",
        unscaled.astype(jnp.bfloat16),
        value_rows,
        preferred_element_type=jnp.float32,
    )
    return (new_peak, totals, weighted)


def empty_state(length, kv_count, group_size):
    return (
        jnp.full((length, kv_count, group_size), lowest, jnp.float32),
        jnp.zeros((length, kv_count, group_size), jnp.float32),
        jnp.zeros((length, kv_count, group_size, HD), jnp.float32),
    )


def local(
    lin_query, lin_key, lin_value, log_decay, out_gate, norm_gain, soft_query, soft_key, soft_value
):
    length = lin_query.shape[1]
    head_count = log_decay.shape[2]
    kv_count = soft_key.shape[2] // HD
    group_size = HEADS // KV_HEADS
    position = lax.axis_index("ctx")
    local_part, carried, closing, device_log = lightning_local(
        lin_query[0], lin_key[0], lin_value[0], log_decay[0]
    )
    gathered_states, device_logs = (
        lax.all_gather(closing[None], "ctx", axis=0, tiled=True),
        lax.all_gather(device_log[None, :], "ctx", axis=0, tiled=True),
    )
    devices = device_logs.shape[0]
    rising = jnp.cumsum(device_logs, axis=0)
    owners = lax.iota(jnp.int32, devices)
    earlier_mask = (owners < position)[:, None]
    reached = jnp.sum(jnp.where(earlier_mask, device_logs, 0.0), axis=0)
    weight = jnp.where(
        earlier_mask, jnp.exp(jnp.where(earlier_mask, reached[None, :] - rising, 0.0)), 0.0
    )
    incoming = jnp.einsum("jh,jhde->hde", weight, gathered_states, precision=lax.Precision.HIGHEST)
    arrived = jnp.einsum("bthd,hde->bthe", carried, incoming, precision=lax.Precision.HIGHEST)
    mixture = (local_part + arrived).reshape(length, head_count, HD)
    normed = mixture * lax.rsqrt(jnp.mean(mixture * mixture, axis=-1, keepdims=True) + epsilon)
    lin_out = (
        normed.reshape(length, head_count * HD)
        * norm_gain[0][None, :]
        * jax.nn.sigmoid(out_gate[0].astype(jnp.float32))
    ).astype(jnp.bfloat16)
    query_rows = soft_query[0].reshape(length, kv_count, group_size, HD)
    key_rows = soft_key[0].reshape(length, kv_count, HD)
    value_rows = soft_value[0].reshape(length, kv_count, HD)
    row_pos = position * length + lax.iota(jnp.int32, length)
    last_row = position * length + length - 1
    key_piece = lax.all_gather(key_rows, "ctx", axis=0, tiled=True)
    value_piece = lax.all_gather(value_rows, "ctx", axis=0, tiled=True)
    piece_rows = key_piece.shape[0]
    stride = math.gcd(piece_rows, 512)

    def absorb_block(turn, kept):
        offset = turn * stride
        key_part = lax.dynamic_slice_in_dim(key_piece, offset, stride, 0)
        value_part = lax.dynamic_slice_in_dim(value_piece, offset, stride, 0)
        key_pos = offset + lax.iota(jnp.int32, stride)
        return absorb(kept, query_rows, row_pos, key_part, value_part, key_pos)

    def work_all(kept):
        return lax.fori_loop(0, piece_rows // stride, absorb_block, kept)

    def skip_all(kept):
        return kept

    row_peak, totals, weighted = lax.cond(
        jnp.int32(0) <= last_row, work_all, skip_all, empty_state(length, kv_count, group_size)
    )
    soft_out = (weighted / totals[..., None]).astype(jnp.bfloat16).reshape(length, head_count * HD)
    lin_handed, soft_handed = passed_along((lin_out[None], soft_out[None]), "pp", 1)
    return (lin_handed, soft_handed)


def solution(mesh):
    return jax.shard_map(
        local,
        mesh=mesh,
        in_specs=(
            P("pp", "ctx", "tp"),
            P("pp", "ctx", "tp"),
            P("pp", "ctx", "tp"),
            P("pp", "ctx", "tp"),
            P("pp", "ctx", "tp"),
            P("pp", "tp"),
            P("pp", "ctx", "tp"),
            P("pp", "ctx", "tp"),
            P("pp", "ctx", "tp"),
        ),
        out_specs=(P("pp", "ctx", "tp"), P("pp", "ctx", "tp")),
        check_vma=False,
    )
```

profile of v0, /device:TPU:0, one launch (start us, length us, event | category | flops | bytes accessed | tf_op | source)
XLA Modules:
  0.0 104.8 jit_solution(13572819028677515258)
XLA Ops:
  9.3 1.5 %copy.98 = bf16[1,256,2048]{1,2,0:T(8,128)(2,1)S(1)} copy(bf16[1,256,2048]{2,1,0:T(8,128)(2,1)} %param.12) | data formatting | bytes 2097152 | tf_op jit(solution)/shard_map/reshape.8
  10.8 1.3 %copy.104 = bf16[32,8,16,128]{3,2,1,0:T(8,128)(2,1)} copy(bf16[32,8,16,128]{3,1,2,0:T(8,128)(2,1)S(1)} %bitcast.100) | data formatting | bytes 2097152
  12.1 2.8 %convolution_add_fusion = f32[16,128,128]{2,1,0:T(8,128)} fusion(bf16[256,16,128]{0,2,1:T(8,128)(2,1)S(1)} %bitcast.103, f32[256,16]{0,1:T(8,128)S(1)} %bitcast.113, bf16[256,16,128]{2,1,0:T(8,128)(2,1)} %bitcast.49, f32[16]{0:T(128)S(1)} %get-tuple-element.92), kind=kOutput, calls=%fused_computation.34 | convolution fusion | flops 136052736 | bytes 3162176 | tf_op jit(solution)/shard_map/bshd,bshe->bhde/dot_general | solution.py:39
  15.3 7.1 %all_gather.14 = bf16[512,2,128]{0,2,1:T(8,128)(2,1)S(1)} all-gather(bf16[256,2,128]{0,2,1:T(8,128)(2,1)S(1)} %bitcast.106), channel_id=1, replica_groups=mesh['ctx'=2,'tp'=4,'pp'=4] {'ctx'}, dimensions={0}, use_global_device_ids=true | all-gather | bytes 393216 | tf_op jit(solution)/shard_map/all_gather | solution.py:120
  22.4 7.4 %all_gather.15 = bf16[512,2,128]{0,2,1:T(8,128)(2,1)S(1)} all-gather(bf16[256,2,128]{0,2,1:T(8,128)(2,1)S(1)} %bitcast.105), channel_id=1, replica_groups=mesh['ctx'=2,'tp'=4,'pp'=4] {'ctx'}, dimensions={0}, use_global_device_ids=true | all-gather | bytes 393216 | tf_op jit(solution)/shard_map/all_gather | solution.py:121
  29.7 6.3 %conditional.1 = (f32[256,2,8]{0,2,1:T(8,128)S(1)}, f32[256,2,8,128]{3,0,2,1:T(8,128)S(1)}) conditional(s32[]{:T(128)} %convert_element_type.48, () %tuple.20, (s32[]{:T(128)}, s32[256]{0:T(256)S(1)}, bf16[1,256,2048]{2,1,0:T(8,128)(2,1)S(1)}, bf16[512,2,128]{0,2,1:T(8,128)(2,1)S(1)}, bf16[512,2,128]{0,2,1:T(8,128)(2,1)S(1)}) %tuple.38), branch_computations={%region_5.6_spmd, %region_6.9_spmd} | conditional | flops 1097478400 | bytes 31640596 | solution.py:138
  30.0 1.7 %fusion = (f32[256,2,8]{0,2,1:T(8,128)S(1)}, f32[2,512,256,8]{2,1,3,0:T(8,128)S(1)}) fusion(pred[256,512]{0,1:T(8,128)(4,1)S(1)} %iota_compare_fusion, bf16[256,2,8,128]{3,2,1,0:T(8,128)(2,1)S(1)} %bitcast.98, bf16[512,2,128]{0,2,1:T(8,128)(2,1)S(1)} %get-tuple-element.81), kind=kOutput, calls=%fused_computation.2 | convolution fusion | flops 543158272 | bytes 9846784 | tf_op jit(solution)/shard_map/cond/branch_1_fun/while/body/eval_jaxpr/tkgd,skd->tkgs/dot_general | solution.py:57
  31.7 1.7 %fusion.4 = f32[256,2,8]{0,2,1:T(8,128)S(1)} fusion(f32[2,512,256,8]{2,1,3,0:T(8,128)S(1)} %get-tuple-element.88, f32[256,2,8]{0,2,1:T(8,128)S(1)} %broadcast_maximum_fusion, pred[256,512]{0,1:T(8,128)(4,1)S(1)} %iota_compare_fusion), kind=kLoop, calls=%fused_computation.6 | loop fusion | flops 8384512 | bytes 8552448 | tf_op jit(solution)/shard_map/cond/branch_1_fun/while/body/eval_jaxpr/reduce_sum | solution.py:65
  33.5 2.6 %bitcast_add_fusion = f32[256,2,8,128]{3,0,2,1:T(8,128)S(1)} fusion(f32[2,512,256,8]{2,1,3,0:T(8,128)S(1)} %get-tuple-element.88, f32[256,2,8]{0,2,1:T(8,128)S(1)} %broadcast_maximum_fusion, pred[256,512]{0,1:T(8,128)(4,1)S(1)} %iota_compare_fusion, f32[256,2,8]{0,2,1:T(8,128)S(1)} %get-tuple-element.85, bf16[512,2,128]{0,2,1:T(8,128)(2,1)S(1)} %get-tuple-element.82), kind=kOutput, calls=%fused_computation.9 | convolution fusion | flops 545783808 | bytes 10911744 | tf_op jit(solution)/shard_map/cond/branch_1_fun/while/body/eval_jaxpr/tkgs,skd->tkgd/dot_general | solution.py:66
  37.5 1.3 %broadcast_in_dim_reshape.3 = bf16[1,256,2048]{2,1,0:T(8,128)(2,1)} reshape(bf16[256,2,8,128]{3,2,1,0:T(8,128)(2,1)S(1)} %copy.79) | data formatting | bytes 2097152 | tf_op jit(solution)/shard_map/broadcast_in_dim;reshape | solution.py:142
  38.8 1.3 %collective-permute-start.1 = (bf16[1,256,2048]{2,1,0:T(8,128)(2,1)}, bf16[1,256,2048]{2,1,0:T(8,128)(2,1)}, u32[]{:S(2)}, u32[]{:S(2)}) collective-permute-start(bf16[1,256,2048]{2,1,0:T(8,128)(2,1)} %broadcast_in_dim_reshape.3), channel_id=1, source_target_pairs={{3,0},{0,1},{1,2},{2,3},{7,4},{4,5},{5,6},{6,7},{11,8},{8,9},{9,10... | collective-permute-start | bytes 3145736 | tf_op jit(solution)/shard_map/ppermute | solution.py:18
  40.0 4.8 %all-gather = f32[2,1,16]{2,1,0:T(1,128)S(1)} all-gather(f32[1,1,16]{2,1,0:T(1,128)S(1)} %copy.70), channel_id=2, replica_groups=mesh['ctx'=2,'tp'=4,'pp'=4] {'ctx'}, dimensions={0}, use_global_device_ids=true | all-gather | bytes 192 | tf_op jit(solution)/shard_map/all_gather | solution.py:96
  45.4 4.4 %fusion.20 = f32[16,256,128]{1,2,0:T(8,128)} fusion(bf16[256,16,128]{0,2,1:T(8,128)(2,1)S(1)} %bitcast.104, f32[16,256]{1,0:T(8,128)S(1)} %bitcast_add_fusion.3, pred[256,256]{1,0:T(8,128)(4,1)S(1)} %iota_compare_fusion.1, bf16[256,16,128]{2,1,0:T(8,128)(2,1)} %bitcast.49, bf16[256,16,128]{2,1,0:T(8,128)(2,1)S(1)} %bitcast.94), kind=kOutput, calls=%fused_computation.33 | convolution fusion | flops 542113792 | bytes 5324800 | tf_op jit(solution)/shard_map/bhts,bshd->bthd/dot_general | solution.py:35
  49.8 1.1 %all-gather.4.cloned.1.call-done = f32[32,128,128]{2,1,0:T(8,128)} async-done(((f32[16,128,128]{2,1,0:T(8,128)}), f32[32,128,128]{2,1,0:T(8,128)}) %all-gather.4.cloned.1.call-update) | async-done | bytes 2097168 | tf_op jit(solution)/shard_map/all_gather | solution.py:95
  50.9 1.9 %multiply_reduce_fusion = f32[16,128,128]{2,1,0:T(8,128)S(1)} fusion(f32[16,2,128,128]{3,2,0,1:T(8,128)} %bitcast.99, f32[16,2]{0,1:T(2,128)S(1)} %select_bitcast_fusion), kind=kLoop, calls=%fused_computation.24 | loop fusion | flops 786432 | bytes 3145856 | tf_op jit(solution)/shard_map/jh,jhde->hde/dot_general | solution.py:106
  52.8 3.0 %fusion.17 = f32[16,128,256]{2,1,0:T(8,128)S(1)} fusion(f32[16,128,128]{2,1,0:T(8,128)S(1)} %multiply_reduce_fusion, f32[16]{0:T(128)S(1)} %get-tuple-element.91, f32[256,16]{0,1:T(8,128)S(1)} %bitcast.107, bf16[256,16,128]{2,1,0:T(8,128)(2,1)S(1)} %bitcast.95), kind=kOutput, calls=%fused_computation.28 | convolution fusion | flops 806879232 | bytes 4210752 | tf_op jit(solution)/shard_map/bthd,hde->bthe/dot_general | solution.py:107
  55.8 2.8 %multiply_reduce_fusion.1 = (f32[256,16]{0,1:T(8,128)S(1)}, f32[1,256,16,128]{1,3,2,0:T(8,128)S(1)}) fusion(f32[16,128,256]{2,1,0:T(8,128)S(1)} %fusion.17, f32[256,16]{0,1:T(8,128)S(1)} %bitcast.108, bf16[256,16,128]{2,1,0:T(8,128)(2,1)S(1)} %bitcast.96, f32[16,256,128]{1,2,0:T(8,128)S(1)} %copy-done.2), kind=kOutput, calls=%fused_computation.27 | convolution fusion | flops 808448000 | bytes 7372800 | tf_op jit(solution)/shard_map/bthd,bhde->bthe/dot_general | solution.py:49
  58.6 1.9 %copy.74 = f32[1,256,2048]{2,1,0:T(8,128)} copy(f32[1,256,2048]{1,2,0:T(8,128)S(1)} %bitcast.97) | data formatting | bytes 4194304 | tf_op jit(solution)/shard_map/reshape | solution.py:108
  60.6 1.9 %mul.139 = f32[256,16,128]{2,1,0:T(8,128)} broadcast(f32[256,16]{1,0:T(8,128)S(1)} %copy.73), dimensions={0,1} | broadcast | bytes 2113536 | tf_op jit(solution)/shard_map/mul | solution.py:109
  62.6 2.8 %mul.140 = f32[1,256,2048]{2,1,0:T(8,128)} reshape(f32[256,16,128]{2,1,0:T(8,128)} %mul.139) | data formatting | bytes 4194304 | tf_op jit(solution)/shard_map/mul | solution.py:109
  65.4 2.2 %multiply_convert_fusion.1 = bf16[1,256,2048]{2,1,0:T(8,128)(2,1)S(1)} fusion(bf16[1,256,2048]{2,1,0:T(8,128)(2,1)S(1)} %copy-done.8, f32[1,256,2048]{2,1,0:T(8,128)S(1)} %copy-done.1, f32[1,256,2048]{2,1,0:T(8,128)} %mul.140, f32[2048]{0:T(1024)S(1)} %bitcast.114), kind=kLoop, calls=%fused_computation.26 | loop fusion | flops 4194304 | bytes 6299648 | tf_op jit(solution)/shard_map/convert_element_type | solution.py:114
  67.6 1.7 %collective-permute-start = (bf16[1,256,2048]{2,1,0:T(8,128)(2,1)S(1)}, bf16[1,256,2048]{2,1,0:T(8,128)(2,1)S(1)}, u32[]{:S(2)}, u32[]{:S(2)}) collective-permute-start(bf16[1,256,2048]{2,1,0:T(8,128)(2,1)S(1)} %multiply_convert_fusion.1), channel_id=1, source_target_pairs={{3,0},{0,1},{1,2},{2,3},{7,4},{4,5},{5,6},{6,7},{11,8},{8,9},{9,10... | collective-permute-start | bytes 3145736 | tf_op jit(solution)/shard_map/ppermute | solution.py:18
  69.3 25.4 %collective-permute-done = bf16[1,256,2048]{2,1,0:T(8,128)(2,1)S(1)} collective-permute-done((bf16[1,256,2048]{2,1,0:T(8,128)(2,1)S(1)}, bf16[1,256,2048]{2,1,0:T(8,128)(2,1)S(1)}, u32[]{:S(2)}, u32[]{:S(2)}) %collective-permute-start) | collective-permute-done | bytes 1048608 | tf_op jit(solution)/shard_map/ppermute | solution.py:18
  95.6 2.3 %copy.140 = bf16[1,256,2048]{2,1,0:T(8,128)(2,1)} copy(bf16[1,256,2048]{2,1,0:T(8,128)(2,1)} %collective-permute-done.1) | data formatting | bytes 2097152
  (63 shorter events, 5.7 us)
Async XLA Ops:
  7.2 0.7 copy-start
  7.2 3.6 %copy-start.3 = (bf16[1,256,2048]{2,1,0:T(8,128)(2,1)S(1)}, bf16[1,256,2048]{2,1,0:T(8,128)(2,1)}, u32[]{:S(2)}) copy-start(bf16[1,256,2048]{2,1,0:T(8,128)(2,1)} %param.13) | copy-start | bytes 3145732
  7.2 43.7 %all-gather.4.cloned.1.call-start = ((), (), s32[]{:S(2)}) async-start(), calls=%async_computation | async-start | bytes 3145728 | tf_op jit(solution)/shard_map/all_gather | solution.py:95
  10.8 4.1 %copy-start.6 = (bf16[1,256,2048]{1,2,0:T(8,128)(2,1)}, bf16[1,256,2048]{1,2,0:T(8,128)(2,1)S(1)}, u32[]{:S(2)}) copy-start(bf16[1,256,2048]{1,2,0:T(8,128)(2,1)S(1)} %copy.98) | copy-start | bytes 3145732
  12.1 2.9 %copy-start.9 = (bf16[1,256,256]{2,1,0:T(8,128)(2,1)S(1)}, bf16[1,256,256]{2,1,0:T(8,128)(2,1)}, u32[]{:S(2)}) copy-start(bf16[1,256,256]{2,1,0:T(8,128)(2,1)} %param.18) | copy-start | bytes 393220
  12.1 3.0 %copy-start.10 = (bf16[1,256,256]{2,1,0:T(8,128)(2,1)S(1)}, bf16[1,256,256]{2,1,0:T(8,128)(2,1)}, u32[]{:S(2)}) copy-start(bf16[1,256,256]{2,1,0:T(8,128)(2,1)} %param.19) | copy-start | bytes 393220
  12.1 17.6 %copy-start.4 = (bf16[1,256,2048]{2,1,0:T(8,128)(2,1)S(1)}, bf16[1,256,2048]{2,1,0:T(8,128)(2,1)}, u32[]{:S(2)}) copy-start(bf16[1,256,2048]{2,1,0:T(8,128)(2,1)} %param.17) | copy-start | bytes 3145732
  36.8 8.1 %copy-start.5 = (bf16[1,256,2048]{2,1,0:T(8,128)(2,1)S(1)}, bf16[1,256,2048]{2,1,0:T(8,128)(2,1)}, u32[]{:S(2)}) copy-start(bf16[1,256,2048]{2,1,0:T(8,128)(2,1)} %param.11) | copy-start | bytes 3145732
  37.5 7.9 %copy-start.7 = (bf16[1,256,2048]{1,2,0:T(8,128)(2,1)S(1)}, bf16[1,256,2048]{1,2,0:T(8,128)(2,1)}, u32[]{:S(2)}) copy-start(bf16[1,256,2048]{1,2,0:T(8,128)(2,1)} %copy-done.6) | copy-start | bytes 3145732
  38.8 30.5 %collective-permute-start.1 = (bf16[1,256,2048]{2,1,0:T(8,128)(2,1)}, bf16[1,256,2048]{2,1,0:T(8,128)(2,1)}, u32[]{:S(2)}, u32[]{:S(2)}) collective-permute-start(bf16[1,256,2048]{2,1,0:T(8,128)(2,1)} %broadcast_in_dim_reshape.3), channel_id=1, source_target_pairs={{3,0},{0,1},{1,2},{2,3},{7,4},{4,5},{5,6},{6,7},{11,8},{8,9},{9,10... | collective-permute-start | bytes 3145736 | tf_op jit(solution)/shard_map/ppermute | solution.py:18
  52.8 3.0 %copy-start.2 = (f32[16,256,128]{1,2,0:T(8,128)S(1)}, f32[16,256,128]{1,2,0:T(8,128)}, u32[]{:S(2)}) copy-start(f32[16,256,128]{1,2,0:T(8,128)} %fusion.20) | copy-start | bytes 6291460
  62.5 2.8 %copy-start.1 = (f32[1,256,2048]{2,1,0:T(8,128)S(1)}, f32[1,256,2048]{2,1,0:T(8,128)}, u32[]{:S(2)}) copy-start(f32[1,256,2048]{2,1,0:T(8,128)} %copy.74) | copy-start | bytes 6291460
  62.5 2.8 %copy-start.8 = (bf16[1,256,2048]{2,1,0:T(8,128)(2,1)S(1)}, bf16[1,256,2048]{2,1,0:T(8,128)(2,1)}, u32[]{:S(2)}) copy-start(bf16[1,256,2048]{2,1,0:T(8,128)(2,1)} %param.15) | copy-start | bytes 3145732
  62.6 2.8 %copy-start.11 = (f32[1,2048]{1,0:T(1,128)S(1)}, f32[1,2048]{1,0:T(1,128)}, u32[]{:S(2)}) copy-start(f32[1,2048]{1,0:T(1,128)} %param.16) | copy-start | bytes 24580
  67.6 27.1 %collective-permute-start = (bf16[1,256,2048]{2,1,0:T(8,128)(2,1)S(1)}, bf16[1,256,2048]{2,1,0:T(8,128)(2,1)S(1)}, u32[]{:S(2)}, u32[]{:S(2)}) collective-permute-start(bf16[1,256,2048]{2,1,0:T(8,128)(2,1)S(1)} %multiply_convert_fusion.1), channel_id=1, source_target_pairs={{3,0},{0,1},{1,2},{2,3},{7,4},{4,5},{5,6},{6,7},{11,8},{8,9},{9,10... | collective-permute-start | bytes 3145736 | tf_op jit(solution)/shard_map/ppermute | solution.py:18
Sparse Core Ops, SparseCore 0:
  15.1 35.8 all-gather.3
where the time goes:
time: 105 us
  waiting for transfers between devices  26.6 us (25%)
  blocking collectives  19.3 us (18%)
  matrix products  17.2 us (16%)
  local copies, waits for them, and re-layouts  16.8 us (16%)
  between operations  14.3 us (14%)
  other arithmetic  7.62 us (7%)
  starting transfers between devices  2.99 us (3%)
    ppermute x2, waiting for transfers between devices, passed_along(): return lax.ppermute(block, axis, route)  25.4 us
    all_gather x1, blocking collectives, local(): value_piece = lax.all_gather(value_rows, 'ctx', axis=0, tiled=True)  7.36 us
    all_gather x1, blocking collectives, local(): key_piece = lax.all_gather(key_rows, 'ctx', axis=0, tiled=True)  7.09 us
    unnamed x32, local copies, waits for them, and re-layouts  5.69 us
    all_gather x1, blocking collectives, local(): lax.all_gather(device_log[None, :], 'ctx', axis=0, tiled=True)  4.82 us
    mul x2, local copies, waits for them, and re-layouts, local(): mixture * lax.rsqrt(jnp.mean(mixture * mixture, axis=-1, keepdims=True) +...  4.77 us
    dot_general x1, matrix products, lightning_local(): jnp.einsum('bhts,bshd->bthd', weights, values_all, preferred_element_type...  4.43 us
    dot_general x1, matrix products, local(): jnp.einsum('bthd,hde->bthe', carried, incoming, precision=lax.Precision.H...  2.96 us
  transfers between devices with their start and end apart: 3, of which 2 were waited for; matrix products, arithmetic and copies ran while one was open for 29% of the time, Pallas kernels for 0%

commit v1 on v0

--- a/solution.py
+++ b/solution.py
@@ -117,8 +117,11 @@
     value_rows = soft_value[0].reshape(length, kv_count, HD)
     row_pos = position * length + lax.iota(jnp.int32, length)
     last_row = position * length + length - 1
-    key_piece = lax.all_gather(key_rows, "ctx", axis=0, tiled=True)
-    value_piece = lax.all_gather(value_rows, "ctx", axis=0, tiled=True)
+    key_piece, value_piece = jnp.split(
+        lax.all_gather(jnp.concatenate([key_rows, value_rows], axis=1), "ctx", axis=0, tiled=True),
+        [key_rows.shape[1]],
+        axis=1,
+    )
     piece_rows = key_piece.shape[0]
     stride = math.gcd(piece_rows, 512)
 

time: 105 us -> 105 us (level)
  blocking collectives: 19.3 us -> 14.3 us
  waiting for transfers between devices: 26.6 us -> 30.7 us
    all_gather x2 -> x1, blocking collectives: 14.5 us -> 9.91 us  [local(): lax.all_gather(jnp.concatenate([key_rows, value_rows], axis=1), 'ctx', ax...]
    all_gather x1, waiting for transfers between devices: 1.15 us -> 5.45 us  [local(): lax.all_gather(closing[None], 'ctx', axis=0, tiled=True)]
  transfers between devices with their start and end apart: 3 -> 3, of which waited for: 2 -> 2; matrix products, arithmetic and copies ran while one was open for 29% -> 30% of each run, Pallas kernels for 0% -> 0%
where the time goes in v1:
time: 105 us; the launch traced here: 104 us
  waiting for transfers between devices  30.7 us (29%)
  local copies, waits for them, and re-layouts  17.1 us (16%)
  matrix products  17 us (16%)
  blocking collectives  14.3 us (14%)
  between operations  14.3 us (14%)
  other arithmetic  7.65 us (7%)
  starting transfers between devices  3.41 us (3%)
    ppermute x2, waiting for transfers between devices, passed_along(): return lax.ppermute(block, axis, route)  25.2 us
    all_gather x1, blocking collectives, local(): lax.all_gather(jnp.concatenate([key_rows, value_rows], axis=1), 'ctx', ax...  9.91 us
    unnamed x32, local copies, waits for them, and re-layouts  5.69 us
    all_gather x1, waiting for transfers between devices, local(): lax.all_gather(closing[None], 'ctx', axis=0, tiled=True)  5.45 us
    mul x2, local copies, waits for them, and re-layouts, local(): mixture * lax.rsqrt(jnp.mean(mixture * mixture, axis=-1, keepdims=True) +...  4.77 us
    dot_general x1, matrix products, lightning_local(): jnp.einsum('bhts,bshd->bthd', weights, values_all, preferred_element_type...  4.43 us
    all_gather x1, blocking collectives, local(): lax.all_gather(device_log[None, :], 'ctx', axis=0, tiled=True)  4.39 us
    ppermute x2, starting transfers between devices, passed_along(): return lax.ppermute(block, axis, route)  3.37 us
  transfers between devices with their start and end apart: 3, of which 2 were waited for; matrix products, arithmetic and copies ran while one was open for 30% of the time, Pallas kernels for 0%

profile of v1, /device:TPU:0, one launch (start us, length us, event | category | flops | bytes accessed | tf_op | source)
XLA Modules:
  0.0 104.4 jit_solution(17386262384960449618)
XLA Ops:
  9.3 1.5 %copy.91 = bf16[1,256,2048]{1,2,0:T(8,128)(2,1)S(1)} copy(bf16[1,256,2048]{2,1,0:T(8,128)(2,1)} %param.12) | data formatting | bytes 2097152 | tf_op jit(solution)/shard_map/reshape.8
  10.8 1.3 %copy.97 = bf16[32,8,16,128]{3,2,1,0:T(8,128)(2,1)} copy(bf16[32,8,16,128]{3,1,2,0:T(8,128)(2,1)S(1)} %bitcast.100) | data formatting | bytes 2097152
  12.1 2.8 %convolution_add_fusion = f32[16,128,128]{2,1,0:T(8,128)} fusion(bf16[256,16,128]{0,2,1:T(8,128)(2,1)S(1)} %bitcast.103, f32[256,16]{0,1:T(8,128)S(1)} %bitcast.113, bf16[256,16,128]{2,1,0:T(8,128)(2,1)} %bitcast.49, f32[16]{0:T(128)S(1)} %get-tuple-element.89), kind=kOutput, calls=%fused_computation.34 | convolution fusion | flops 136052736 | bytes 3162176 | tf_op jit(solution)/shard_map/bshd,bshe->bhde/dot_general | solution.py:39
  15.2 9.9 %all_gather.11 = bf16[512,4,128]{0,2,1:T(8,128)(2,1)S(1)} all-gather(bf16[256,4,128]{0,2,1:T(8,128)(2,1)S(1)} %pad_maximum_fusion), channel_id=1, replica_groups=mesh['ctx'=2,'tp'=4,'pp'=4] {'ctx'}, dimensions={0}, use_global_device_ids=true | all-gather | bytes 786432 | tf_op jit(solution)/shard_map/all_gather | solution.py:121
  25.1 6.4 %conditional.1 = (f32[256,2,8]{0,2,1:T(8,128)S(1)}, f32[256,2,8,128]{3,0,2,1:T(8,128)S(1)}) conditional(s32[]{:T(128)} %convert_element_type.48, () %tuple.20, (s32[]{:T(128)}, s32[256]{0:T(256)S(1)}, bf16[512,4,128]{0,2,1:T(8,128)(2,1)S(1)}, bf16[1,256,2048]{2,1,0:T(8,128)(2,1)S(1)}) %tuple.38), branch_computations={%region_5.6_spmd, %region_6.9_spmd} | conditional | flops 1097478400 | bytes 32689172 | solution.py:141
  25.8 1.5 %fusion = (f32[256,2,8]{0,2,1:T(8,128)S(1)}, f32[2,512,256,8]{2,1,3,0:T(8,128)S(1)}) fusion(pred[256,512]{0,1:T(8,128)(4,1)S(1)} %iota_compare_fusion, bf16[256,2,8,128]{3,2,1,0:T(8,128)(2,1)S(1)} %bitcast.98, bf16[512,4,128]{2,0,1:T(8,128)(2,1)S(1)} %copy.75), kind=kOutput, calls=%fused_computation.2 | convolution fusion | flops 543158272 | bytes 9846784 | tf_op jit(solution)/shard_map/cond/branch_1_fun/while/body/eval_jaxpr/tkgd,skd->tkgs/dot_general | solution.py:57
  27.3 1.7 %fusion.4 = f32[256,2,8]{0,2,1:T(8,128)S(1)} fusion(f32[2,512,256,8]{2,1,3,0:T(8,128)S(1)} %get-tuple-element.85, f32[256,2,8]{0,2,1:T(8,128)S(1)} %broadcast_maximum_fusion, pred[256,512]{0,1:T(8,128)(4,1)S(1)} %iota_compare_fusion), kind=kLoop, calls=%fused_computation.6 | loop fusion | flops 8384512 | bytes 8552448 | tf_op jit(solution)/shard_map/cond/branch_1_fun/while/body/eval_jaxpr/reduce_sum | solution.py:65
  29.0 2.5 %bitcast_add_fusion = f32[256,2,8,128]{3,0,2,1:T(8,128)S(1)} fusion(f32[2,512,256,8]{2,1,3,0:T(8,128)S(1)} %get-tuple-element.85, f32[256,2,8]{0,2,1:T(8,128)S(1)} %broadcast_maximum_fusion, pred[256,512]{0,1:T(8,128)(4,1)S(1)} %iota_compare_fusion, f32[256,2,8]{0,2,1:T(8,128)S(1)} %get-tuple-element.82, bf16[512,4,128]{2,0,1:T(8,128)(2,1)S(1)} %copy.75), kind=kOutput, calls=%fused_computation.9 | convolution fusion | flops 545783808 | bytes 10911744 | tf_op jit(solution)/shard_map/cond/branch_1_fun/while/body/eval_jaxpr/tkgs,skd->tkgd/dot_general | solution.py:66
  33.0 1.3 %broadcast_in_dim_reshape.3 = bf16[1,256,2048]{2,1,0:T(8,128)(2,1)} reshape(bf16[256,2,8,128]{3,2,1,0:T(8,128)(2,1)S(1)} %copy.76) | data formatting | bytes 2097152 | tf_op jit(solution)/shard_map/broadcast_in_dim;reshape | solution.py:145
  34.3 1.8 %collective-permute-start.1 = (bf16[1,256,2048]{2,1,0:T(8,128)(2,1)}, bf16[1,256,2048]{2,1,0:T(8,128)(2,1)}, u32[]{:S(2)}, u32[]{:S(2)}) collective-permute-start(bf16[1,256,2048]{2,1,0:T(8,128)(2,1)} %broadcast_in_dim_reshape.3), channel_id=1, source_target_pairs={{3,0},{0,1},{1,2},{2,3},{7,4},{4,5},{5,6},{6,7},{11,8},{8,9},{9,10... | collective-permute-start | bytes 3145736 | tf_op jit(solution)/shard_map/ppermute | solution.py:18
  36.1 4.4 %all-gather = f32[2,1,16]{2,1,0:T(1,128)S(1)} all-gather(f32[1,1,16]{2,1,0:T(1,128)S(1)} %copy.68), channel_id=2, replica_groups=mesh['ctx'=2,'tp'=4,'pp'=4] {'ctx'}, dimensions={0}, use_global_device_ids=true | all-gather | bytes 192 | tf_op jit(solution)/shard_map/all_gather | solution.py:96
  41.0 4.4 %fusion.18 = f32[16,256,128]{1,2,0:T(8,128)} fusion(bf16[256,16,128]{0,2,1:T(8,128)(2,1)S(1)} %bitcast.104, f32[16,256]{1,0:T(8,128)S(1)} %bitcast_add_fusion.3, pred[256,256]{1,0:T(8,128)(4,1)S(1)} %iota_compare_fusion.1, bf16[256,16,128]{2,1,0:T(8,128)(2,1)} %bitcast.49, bf16[256,16,128]{2,1,0:T(8,128)(2,1)S(1)} %bitcast.94), kind=kOutput, calls=%fused_computation.33 | convolution fusion | flops 542113792 | bytes 5324800 | tf_op jit(solution)/shard_map/bhts,bshd->bthd/dot_general | solution.py:35
  45.4 5.5 %all-gather.4.cloned.1.call-done = f32[32,128,128]{2,1,0:T(8,128)} async-done(((f32[16,128,128]{2,1,0:T(8,128)}), f32[32,128,128]{2,1,0:T(8,128)}) %all-gather.4.cloned.1.call-update) | async-done | bytes 2097168 | tf_op jit(solution)/shard_map/all_gather | solution.py:95
  50.9 1.9 %multiply_reduce_fusion = f32[16,128,128]{2,1,0:T(8,128)S(1)} fusion(f32[16,2,128,128]{3,2,0,1:T(8,128)} %bitcast.99, f32[16,2]{0,1:T(2,128)S(1)} %select_bitcast_fusion), kind=kLoop, calls=%fused_computation.24 | loop fusion | flops 786432 | bytes 3145856 | tf_op jit(solution)/shard_map/jh,jhde->hde/dot_general | solution.py:106
  52.8 3.0 %fusion.15 = f32[16,128,256]{2,1,0:T(8,128)S(1)} fusion(f32[16,128,128]{2,1,0:T(8,128)S(1)} %multiply_reduce_fusion, f32[16]{0:T(128)S(1)} %get-tuple-element.88, f32[256,16]{0,1:T(8,128)S(1)} %bitcast.107, bf16[256,16,128]{2,1,0:T(8,128)(2,1)S(1)} %bitcast.95), kind=kOutput, calls=%fused_computation.28 | convolution fusion | flops 806879232 | bytes 4210752 | tf_op jit(solution)/shard_map/bthd,hde->bthe/dot_general | solution.py:107
  55.8 2.8 %multiply_reduce_fusion.1 = (f32[256,16]{0,1:T(8,128)S(1)}, f32[1,256,16,128]{1,3,2,0:T(8,128)S(1)}) fusion(f32[16,128,256]{2,1,0:T(8,128)S(1)} %fusion.15, f32[256,16]{0,1:T(8,128)S(1)} %bitcast.108, bf16[256,16,128]{2,1,0:T(8,128)(2,1)S(1)} %bitcast.96, f32[16,256,128]{1,2,0:T(8,128)S(1)} %copy-done.2), kind=kOutput, calls=%fused_computation.27 | convolution fusion | flops 808448000 | bytes 7372800 | tf_op jit(solution)/shard_map/bthd,bhde->bthe/dot_general | solution.py:49
  58.6 1.9 %copy.72 = f32[1,256,2048]{2,1,0:T(8,128)} copy(f32[1,256,2048]{1,2,0:T(8,128)S(1)} %bitcast.97) | data formatting | bytes 4194304 | tf_op jit(solution)/shard_map/reshape | solution.py:108
  60.5 1.9 %mul.139 = f32[256,16,128]{2,1,0:T(8,128)} broadcast(f32[256,16]{1,0:T(8,128)S(1)} %copy.71), dimensions={0,1} | broadcast | bytes 2113536 | tf_op jit(solution)/shard_map/mul | solution.py:109
  62.5 2.8 %mul.140 = f32[1,256,2048]{2,1,0:T(8,128)} reshape(f32[256,16,128]{2,1,0:T(8,128)} %mul.139) | data formatting | bytes 4194304 | tf_op jit(solution)/shard_map/mul | solution.py:109
  65.3 2.2 %multiply_convert_fusion.1 = bf16[1,256,2048]{2,1,0:T(8,128)(2,1)S(1)} fusion(bf16[1,256,2048]{2,1,0:T(8,128)(2,1)S(1)} %copy-done.8, f32[1,256,2048]{2,1,0:T(8,128)S(1)} %copy-done.1, f32[1,256,2048]{2,1,0:T(8,128)} %mul.140, f32[2048]{0:T(1024)S(1)} %bitcast.114), kind=kLoop, calls=%fused_computation.26 | loop fusion | flops 4194304 | bytes 6299648 | tf_op jit(solution)/shard_map/convert_element_type | solution.py:114
  67.5 1.5 %collective-permute-start = (bf16[1,256,2048]{2,1,0:T(8,128)(2,1)S(1)}, bf16[1,256,2048]{2,1,0:T(8,128)(2,1)S(1)}, u32[]{:S(2)}, u32[]{:S(2)}) collective-permute-start(bf16[1,256,2048]{2,1,0:T(8,128)(2,1)S(1)} %multiply_convert_fusion.1), channel_id=1, source_target_pairs={{3,0},{0,1},{1,2},{2,3},{7,4},{4,5},{5,6},{6,7},{11,8},{8,9},{9,10... | collective-permute-start | bytes 3145736 | tf_op jit(solution)/shard_map/ppermute | solution.py:18
  69.1 25.2 %collective-permute-done = bf16[1,256,2048]{2,1,0:T(8,128)(2,1)S(1)} collective-permute-done((bf16[1,256,2048]{2,1,0:T(8,128)(2,1)S(1)}, bf16[1,256,2048]{2,1,0:T(8,128)(2,1)S(1)}, u32[]{:S(2)}, u32[]{:S(2)}) %collective-permute-start) | collective-permute-done | bytes 1048608 | tf_op jit(solution)/shard_map/ppermute | solution.py:18
  94.3 1.0 copy.132
  95.3 2.3 %copy.133 = bf16[1,256,2048]{2,1,0:T(8,128)(2,1)} copy(bf16[1,256,2048]{2,1,0:T(8,128)(2,1)} %collective-permute-done.1) | data formatting | bytes 2097152
  (64 shorter events, 5.0 us)
Async XLA Ops:
  7.2 0.7 copy-start
  7.2 3.6 %copy-start.3 = (bf16[1,256,2048]{2,1,0:T(8,128)(2,1)S(1)}, bf16[1,256,2048]{2,1,0:T(8,128)(2,1)}, u32[]{:S(2)}) copy-start(bf16[1,256,2048]{2,1,0:T(8,128)(2,1)} %param.13) | copy-start | bytes 3145732
  7.2 43.7 %all-gather.4.cloned.1.call-start = ((), (), s32[]{:S(2)}) async-start(), calls=%async_computation | async-start | bytes 3145728 | tf_op jit(solution)/shard_map/all_gather | solution.py:95
  10.8 4.1 %copy-start.6 = (bf16[1,256,2048]{1,2,0:T(8,128)(2,1)}, bf16[1,256,2048]{1,2,0:T(8,128)(2,1)S(1)}, u32[]{:S(2)}) copy-start(bf16[1,256,2048]{1,2,0:T(8,128)(2,1)S(1)} %copy.91) | copy-start | bytes 3145732
  12.1 2.9 %copy-start.9 = (bf16[1,256,256]{2,1,0:T(8,128)(2,1)S(1)}, bf16[1,256,256]{2,1,0:T(8,128)(2,1)}, u32[]{:S(2)}) copy-start(bf16[1,256,256]{2,1,0:T(8,128)(2,1)} %param.19) | copy-start | bytes 393220
  12.1 3.0 %copy-start.10 = (bf16[1,256,256]{2,1,0:T(8,128)(2,1)S(1)}, bf16[1,256,256]{2,1,0:T(8,128)(2,1)}, u32[]{:S(2)}) copy-start(bf16[1,256,256]{2,1,0:T(8,128)(2,1)} %param.18) | copy-start | bytes 393220
  14.9 10.3 %copy-start.4 = (bf16[1,256,2048]{2,1,0:T(8,128)(2,1)S(1)}, bf16[1,256,2048]{2,1,0:T(8,128)(2,1)}, u32[]{:S(2)}) copy-start(bf16[1,256,2048]{2,1,0:T(8,128)(2,1)} %param.17) | copy-start | bytes 3145732
  32.3 8.3 %copy-start.5 = (bf16[1,256,2048]{2,1,0:T(8,128)(2,1)S(1)}, bf16[1,256,2048]{2,1,0:T(8,128)(2,1)}, u32[]{:S(2)}) copy-start(bf16[1,256,2048]{2,1,0:T(8,128)(2,1)} %param.11) | copy-start | bytes 3145732
  33.0 8.0 %copy-start.7 = (bf16[1,256,2048]{1,2,0:T(8,128)(2,1)S(1)}, bf16[1,256,2048]{1,2,0:T(8,128)(2,1)}, u32[]{:S(2)}) copy-start(bf16[1,256,2048]{1,2,0:T(8,128)(2,1)} %copy-done.6) | copy-start | bytes 3145732
  34.3 34.8 %collective-permute-start.1 = (bf16[1,256,2048]{2,1,0:T(8,128)(2,1)}, bf16[1,256,2048]{2,1,0:T(8,128)(2,1)}, u32[]{:S(2)}, u32[]{:S(2)}) collective-permute-start(bf16[1,256,2048]{2,1,0:T(8,128)(2,1)} %broadcast_in_dim_reshape.3), channel_id=1, source_target_pairs={{3,0},{0,1},{1,2},{2,3},{7,4},{4,5},{5,6},{6,7},{11,8},{8,9},{9,10... | collective-permute-start | bytes 3145736 | tf_op jit(solution)/shard_map/ppermute | solution.py:18
  52.8 3.0 %copy-start.2 = (f32[16,256,128]{1,2,0:T(8,128)S(1)}, f32[16,256,128]{1,2,0:T(8,128)}, u32[]{:S(2)}) copy-start(f32[16,256,128]{1,2,0:T(8,128)} %fusion.18) | copy-start | bytes 6291460
  62.5 2.8 %copy-start.1 = (f32[1,256,2048]{2,1,0:T(8,128)S(1)}, f32[1,256,2048]{2,1,0:T(8,128)}, u32[]{:S(2)}) copy-start(f32[1,256,2048]{2,1,0:T(8,128)} %copy.72) | copy-start | bytes 6291460
  62.5 2.8 %copy-start.8 = (bf16[1,256,2048]{2,1,0:T(8,128)(2,1)S(1)}, bf16[1,256,2048]{2,1,0:T(8,128)(2,1)}, u32[]{:S(2)}) copy-start(bf16[1,256,2048]{2,1,0:T(8,128)(2,1)} %param.15) | copy-start | bytes 3145732
  62.5 2.8 %copy-start.11 = (f32[1,2048]{1,0:T(1,128)S(1)}, f32[1,2048]{1,0:T(1,128)}, u32[]{:S(2)}) copy-start(f32[1,2048]{1,0:T(1,128)} %param.16) | copy-start | bytes 24580
  67.5 26.8 %collective-permute-start = (bf16[1,256,2048]{2,1,0:T(8,128)(2,1)S(1)}, bf16[1,256,2048]{2,1,0:T(8,128)(2,1)S(1)}, u32[]{:S(2)}, u32[]{:S(2)}) collective-permute-start(bf16[1,256,2048]{2,1,0:T(8,128)(2,1)S(1)} %multiply_convert_fusion.1), channel_id=1, source_target_pairs={{3,0},{0,1},{1,2},{2,3},{7,4},{4,5},{5,6},{6,7},{11,8},{8,9},{9,10... | collective-permute-start | bytes 3145736 | tf_op jit(solution)/shard_map/ppermute | solution.py:18
Sparse Core Ops, SparseCore 0:
  15.0 35.8 all-gather.3
